TPU v7x, 32 devices: a whole 2x2x4 slice. The times are simulated.
32 devices in a mesh: wide: 16 (over z, x, core), narrow: 2 (over y).
Axes of the slice: x: 2, y: 2, z: 4, core: 2. Of those that a mesh axis runs over, the one named last changes fastest.
Arguments:
- tokens: bfloat16 [16384, 768], P(('wide', 'narrow')), may hold values from -6 to 6
- token_marks: int32 [16384], P(('wide', 'narrow')), may hold values 0 or 1
- crop_lengths: int32 [256], P('wide'), may hold values from 0 to 576, as said below
- bucket_ids: int32 [256], P('wide'), may hold values from 0 to 3
- mask_token: bfloat16 [768], replicated, may hold values from -5 to 5
- norm1_gain: bfloat16 [768], replicated, may hold values from 0.099609375 to 1.8984375
- norm1_bias: bfloat16 [768], replicated, may hold values from -3 to 3
- w_qkv: bfloat16 [3, 768, 768], P(None, None, 'narrow'), may hold values from -0.21875 to 0.21875
- qv_bias: bfloat16 [2, 768], P(None, 'narrow'), may hold values from -3 to 3
- w_proj: bfloat16 [768, 768], P('narrow'), may hold values from -1.75 to 1.75
- proj_bias: bfloat16 [768], replicated, may hold values from -3 to 3
- scale_attn: bfloat16 [768], replicated, may hold values from 0.5 to 1.5
- norm2_gain: bfloat16 [768], replicated, may hold values from 0.099609375 to 1.8984375
- norm2_bias: bfloat16 [768], replicated, may hold values from -3 to 3
- w_fc1: bfloat16 [768, 3072], P(None, 'narrow'), may hold values from -0.21875 to 0.21875
- fc1_bias: bfloat16 [3072], P('narrow'), may hold values from -3 to 3
- w_fc2: bfloat16 [3072, 768], P('narrow'), may hold values from -0.109375 to 0.109375
- fc2_bias: bfloat16 [768], replicated, may hold values from -3 to 3
- scale_mlp: bfloat16 [768], replicated, may hold values from 0.5 to 1.5
- cotangent: bfloat16 [16384, 768], P(('wide', 'narrow')), may hold values from -6 to 6
Outputs:
- output: bfloat16 [16384, 768], P(('wide', 'narrow'))
- grad_tokens: float32 [16384, 768], P(('wide', 'narrow'))
- grad_mask_token: float32 [768], replicated
- grad_norm1_gain: float32 [768], replicated
- grad_norm1_bias: float32 [768], replicated
- grad_qkv: float32 [3, 768, 768], P(None, None, 'narrow')
- grad_qv_bias: float32 [2, 768], P(None, 'narrow')
- grad_proj: float32 [768, 768], P('narrow')
- grad_proj_bias: float32 [768], replicated
- grad_scale_attn: float32 [768], replicated
- grad_norm2_gain: float32 [768], replicated
- grad_norm2_bias: float32 [768], replicated
- grad_fc1: float32 [768, 3072], P(None, 'narrow')
- grad_fc1_bias: float32 [3072], P('narrow')
- grad_fc2: float32 [3072, 768], P('narrow')
- grad_fc2_bias: float32 [768], replicated
- grad_scale_mlp: float32 [768], replicated
Inputs may be any that keep to these rules, and one draw needn't show every extreme that they name: `crop_lengths`: length 0 marks an empty slot. The nonempty slots of a buffer come first, and their padded rows together fill at most 1024; some buffer is filled to exactly 1024 rows. A nonempty crop has more than 48 rows, and its bucket is the smallest of 64, 144, 256, 576 that holds it.
All inputs are finite; a program needn't handle non-finite values. No bound on the sum of `token_marks` on one device may be relied on, other than what follows from the above.
Results may differ from a plain program's by a relative error of at most 0.017.
Values may be sent and summed in bfloat16 or wider, within the bound.
No kernel may reach another device: no remote copies, remote signals or barrier semaphores. Data moves between devices by JAX's collectives and lax.ppermute only.
A program may use at most 128 MiB of HBM per device.

v0:
```python
from functools import partial
import jax
import jax.numpy as jnp
from jax import lax
from jax.sharding import PartitionSpec as P

HEAD_DIM = 64
B0 = 64
B1 = 144
B2 = 256
B3 = 576
epsilon = 1e-06
score_scale = 0.125
masked_score = -1e30


def layer_norm(values_in, norm_gain, norm_shift):
    row_mean = jnp.mean(values_in, axis=-1, keepdims=True)
    centered = values_in - row_mean
    variance = jnp.mean(centered * centered, axis=-1, keepdims=True)
    return centered * lax.rsqrt(variance + epsilon) * norm_gain + norm_shift


def row_layout(lengths, buckets, row_total):
    slot_count = lengths.shape[0]
    bucket_rows = jnp.where(
        buckets == 0, B0, jnp.where(buckets == 1, B1, jnp.where(buckets == 2, B2, B3))
    )
    padded_sizes = jnp.where(lengths > 0, bucket_rows, 0).astype(jnp.int32)
    slot_ends = jnp.cumsum(padded_sizes)
    starts = slot_ends - padded_sizes
    row_ids = jnp.arange(row_total, dtype=jnp.int32)
    crop_of_row = jnp.sum((row_ids[:, None] >= slot_ends[None, :]).astype(jnp.int32), axis=1)
    slot_match = crop_of_row[:, None] == jnp.arange(slot_count, dtype=jnp.int32)[None, :]
    row_start = jnp.sum(jnp.where(slot_match, starts[None, :], 0), axis=1)
    row_length = jnp.sum(jnp.where(slot_match, lengths[None, :], 0), axis=1)
    is_valid = (crop_of_row < slot_count) & (row_ids - row_start < row_length)
    return (crop_of_row, is_valid)


def allowed_block(crop_of_row, is_valid, first_row, block_rows):
    row_total = crop_of_row.shape[0]
    query_crop = lax.dynamic_slice_in_dim(crop_of_row, first_row, block_rows)
    query_valid = lax.dynamic_slice_in_dim(is_valid, first_row, block_rows)
    query_ids = first_row + jnp.arange(block_rows, dtype=jnp.int32)
    key_ids = jnp.arange(row_total, dtype=jnp.int32)
    same_crop = (
        (query_crop[:, None] == crop_of_row[None, :]) & query_valid[:, None] & is_valid[None, :]
    )
    itself = (query_ids[:, None] == key_ids[None, :]) & jnp.logical_not(query_valid)[:, None]
    return same_crop | itself


def block_rows_for():
    return 512


def slab(matrix, first_row, row_count):
    return lax.dynamic_slice_in_dim(matrix, first_row, row_count, 0)


def shards(
    tokens,
    token_marks,
    crop_lengths,
    bucket_ids,
    mask_token,
    norm1_gain,
    norm1_bias,
    w_qkv,
    qv_bias,
    w_proj,
    proj_bias,
    scale_attn,
    norm2_gain,
    norm2_bias,
    w_fc1,
    fc1_bias,
    w_fc2,
    fc2_bias,
    scale_mlp,
    cotangent,
):
    own_rows = tokens.shape[0]
    row_total = own_rows * lax.axis_size("narrow")
    first_own = lax.axis_index("narrow") * own_rows
    crop_of_row, is_valid = row_layout(crop_lengths, bucket_ids, row_total)
    own_valid = lax.dynamic_slice_in_dim(is_valid, first_own, own_rows)[:, None]
    marked = (token_marks == 1)[:, None]
    gain1 = norm1_gain.astype(jnp.float32)
    shift1 = norm1_bias.astype(jnp.float32)
    gain2 = norm2_gain.astype(jnp.float32)
    shift2 = norm2_bias.astype(jnp.float32)
    scale1 = scale_attn.astype(jnp.float32)
    scale2 = scale_mlp.astype(jnp.float32)
    x_in = jnp.where(marked, mask_token.astype(jnp.float32)[None, :], tokens.astype(jnp.float32))
    normed1 = layer_norm(x_in, gain1, shift1).astype(jnp.bfloat16)
    normed1_all = lax.all_gather(normed1, "narrow", axis=0, tiled=True)
    projected = jnp.einsum("rd,cde->cre", normed1_all, w_qkv, preferred_element_type=jnp.float32)
    bias_pair = qv_bias.astype(jnp.float32)
    queries = (projected[0] + bias_pair[0]).astype(jnp.bfloat16)
    keys_all = projected[1].astype(jnp.bfloat16)
    values_all = (projected[2] + bias_pair[1]).astype(jnp.bfloat16)
    heads_local = queries.shape[1] // HEAD_DIM
    query_heads = queries.reshape(row_total, heads_local, HEAD_DIM)
    key_heads = keys_all.reshape(row_total, heads_local, HEAD_DIM)
    value_heads = values_all.reshape(row_total, heads_local, HEAD_DIM)
    block_rows = block_rows_for()
    block_count = row_total // block_rows
    block_ids = jnp.arange(block_count, dtype=jnp.int32)

    def attend(block_index):
        first_row = block_index * block_rows
        query_block = slab(query_heads, first_row, block_rows)
        scores = (
            jnp.einsum("qhd,khd->hqk", query_block, key_heads, preferred_element_type=jnp.float32)
            * score_scale
        )
        allowed = allowed_block(crop_of_row, is_valid, first_row, block_rows)
        scores = jnp.where(allowed[None], scores, masked_score)
        row_peak = jnp.max(scores, axis=-1, keepdims=True)
        exponent = jnp.exp(scores - row_peak)
        denominator = jnp.sum(exponent, axis=-1, keepdims=True)
        probability = (exponent / denominator).astype(jnp.bfloat16)
        mixed = jnp.einsum(
            "hqk,khd->qhd", probability, value_heads, preferred_element_type=jnp.float32
        ).astype(jnp.bfloat16)
        return (mixed, (row_peak + jnp.log(denominator))[..., 0])

    mixed_blocks, log_totals = lax.map(attend, block_ids)
    heads_out = mixed_blocks.reshape(row_total, heads_local * HEAD_DIM)
    attn_out = lax.psum_scatter(
        jnp.dot(
            slab(heads_out, jnp.int32(0), own_rows * lax.axis_size("narrow")),
            w_proj,
            preferred_element_type=jnp.float32,
        ).astype(jnp.bfloat16),
        "narrow",
        scatter_dimension=0,
        tiled=True,
    ).astype(jnp.float32) + proj_bias.astype(jnp.float32)
    hidden = x_in + scale1 * attn_out
    normed2 = layer_norm(hidden, gain2, shift2).astype(jnp.bfloat16)
    normed2_all = lax.all_gather(normed2, "narrow", axis=0, tiled=True)
    pre_act = jnp.dot(normed2_all, w_fc1, preferred_element_type=jnp.float32) + fc1_bias.astype(
        jnp.float32
    )
    gelu_exact = partial(jax.nn.gelu, approximate=False)
    activated = gelu_exact(pre_act).astype(jnp.bfloat16)
    branch = lax.psum_scatter(
        jnp.dot(
            slab(activated, jnp.int32(0), own_rows * lax.axis_size("narrow")),
            w_fc2,
            preferred_element_type=jnp.float32,
        ).astype(jnp.bfloat16),
        "narrow",
        scatter_dimension=0,
        tiled=True,
    ).astype(jnp.float32) + fc2_bias.astype(jnp.float32)
    output = jnp.where(own_valid, hidden + scale2 * branch, 0.0).astype(jnp.bfloat16)
    grad_out = jnp.where(own_valid, cotangent.astype(jnp.float32), 0.0)
    grad_branch = (scale2 * grad_out).astype(jnp.bfloat16)
    grad_scale_mlp = jnp.sum(grad_out * branch, axis=0)
    grad_fc2_bias = jnp.sum(grad_branch.astype(jnp.float32), axis=0)
    grad_branch_all = lax.all_gather(grad_branch, "narrow", axis=0, tiled=True)
    grad_fc2 = jnp.einsum(
        "rf,rd->fd", activated, grad_branch_all, preferred_element_type=jnp.float32
    )
    grad_act = jnp.einsum("rd,fd->rf", grad_branch_all, w_fc2, preferred_element_type=jnp.float32)
    gelu_unused, gelu_back = jax.vjp(gelu_exact, pre_act)
    grad_pre = gelu_back(grad_act)[0].astype(jnp.bfloat16)
    grad_fc1_bias = jnp.sum(grad_pre.astype(jnp.float32), axis=0)
    grad_fc1 = jnp.einsum("rd,rf->df", normed2_all, grad_pre, preferred_element_type=jnp.float32)
    grad_normed2 = lax.psum_scatter(
        jnp.einsum(
            "rf,df->rd",
            slab(grad_pre, jnp.int32(0), own_rows * lax.axis_size("narrow")),
            w_fc1,
            preferred_element_type=jnp.float32,
        ).astype(jnp.bfloat16),
        "narrow",
        scatter_dimension=0,
        tiled=True,
    ).astype(jnp.float32)
    norm2_unused, norm2_back = jax.vjp(layer_norm, hidden, gain2, shift2)
    grad_hidden_part, grad_norm2_gain, grad_norm2_bias = norm2_back(grad_normed2)
    grad_hidden = grad_out + grad_hidden_part
    grad_attn = (scale1 * grad_hidden).astype(jnp.bfloat16)
    grad_scale_attn = jnp.sum(grad_hidden * attn_out, axis=0)
    grad_proj_bias = jnp.sum(grad_attn.astype(jnp.float32), axis=0)
    grad_attn_all = lax.all_gather(grad_attn, "narrow", axis=0, tiled=True)
    grad_proj = jnp.einsum(
        "re,rd->ed", heads_out, grad_attn_all, preferred_element_type=jnp.float32
    )
    grad_heads = jnp.einsum(
        "rd,ed->re", grad_attn_all, w_proj, preferred_element_type=jnp.float32
    ).astype(jnp.bfloat16)
    grad_heads = grad_heads.reshape(row_total, heads_local, HEAD_DIM)

    def attend_back(carried, block_index):
        key_sum, value_sum = carried
        first_row = block_index * block_rows
        query_block = slab(query_heads, first_row, block_rows)
        grad_block = slab(grad_heads, first_row, block_rows)
        log_block = log_totals[block_index]
        scores = (
            jnp.einsum("qhd,khd->hqk", query_block, key_heads, preferred_element_type=jnp.float32)
            * score_scale
        )
        allowed = allowed_block(crop_of_row, is_valid, first_row, block_rows)
        exact_probs = jnp.where(
            allowed[None],
            jnp.exp(jnp.where(allowed[None], scores, masked_score) - log_block[..., None]),
            0.0,
        )
        rounded = exact_probs.astype(jnp.bfloat16)
        value_sum = value_sum + jnp.einsum(
            "hqk,qhd->khd", rounded, grad_block, preferred_element_type=jnp.float32
        )
        grad_probs = jnp.einsum(
            "qhd,khd->hqk", grad_block, value_heads, preferred_element_type=jnp.float32
        )
        row_inner = jnp.sum(exact_probs * grad_probs, axis=-1, keepdims=True)
        grad_scores = (exact_probs * (grad_probs - row_inner)).astype(jnp.bfloat16)
        grad_query = (
            jnp.einsum("hqk,khd->qhd", grad_scores, key_heads, preferred_element_type=jnp.float32)
            * score_scale
        )
        key_sum = (
            key_sum
            + jnp.einsum(
                "hqk,qhd->khd", grad_scores, query_block, preferred_element_type=jnp.float32
            )
            * score_scale
        )
        return ((key_sum, value_sum), grad_query)

    zero_heads = jnp.zeros((row_total, heads_local, HEAD_DIM), jnp.float32)
    (key_sum, value_sum), query_blocks = lax.scan(attend_back, (zero_heads, zero_heads), block_ids)
    width_local = heads_local * HEAD_DIM
    grad_queries = query_blocks.reshape(row_total, width_local).astype(jnp.bfloat16)
    grad_keys = key_sum.reshape(row_total, width_local).astype(jnp.bfloat16)
    grad_values = value_sum.reshape(row_total, width_local).astype(jnp.bfloat16)
    grad_stack = jnp.stack([grad_queries, grad_keys, grad_values])
    grad_qkv = jnp.einsum(
        "rd,cre->cde", normed1_all, grad_stack, preferred_element_type=jnp.float32
    )
    grad_qv_bias = jnp.stack(
        [
            jnp.sum(grad_queries.astype(jnp.float32), axis=0),
            jnp.sum(grad_values.astype(jnp.float32), axis=0),
        ]
    )
    grad_qkv, grad_qv_bias, grad_proj, grad_fc1, grad_fc1_bias, grad_fc2 = lax.psum(
        (grad_qkv, grad_qv_bias, grad_proj, grad_fc1, grad_fc1_bias, grad_fc2), "wide"
    )
    grad_normed1 = lax.psum_scatter(
        jnp.einsum("cre,cde->rd", grad_stack, w_qkv, preferred_element_type=jnp.float32).astype(
            jnp.bfloat16
        ),
        "narrow",
        scatter_dimension=0,
        tiled=True,
    ).astype(jnp.float32)
    norm1_unused, norm1_back = jax.vjp(layer_norm, x_in, gain1, shift1)
    grad_x_part, grad_norm1_gain, grad_norm1_bias = norm1_back(grad_normed1)
    grad_x_in = grad_hidden + grad_x_part
    grad_tokens = jnp.where(marked, 0.0, grad_x_in)
    grad_mask_token = jnp.sum(jnp.where(marked, grad_x_in, 0.0), axis=0)
    (
        grad_mask_token,
        grad_norm1_gain,
        grad_norm1_bias,
        grad_proj_bias,
        grad_scale_attn,
        grad_norm2_gain,
        grad_norm2_bias,
        grad_fc2_bias,
        grad_scale_mlp,
    ) = lax.psum(
        (
            grad_mask_token,
            grad_norm1_gain,
            grad_norm1_bias,
            grad_proj_bias,
            grad_scale_attn,
            grad_norm2_gain,
            grad_norm2_bias,
            grad_fc2_bias,
            grad_scale_mlp,
        ),
        ("wide", "narrow"),
    )
    return (
        output,
        grad_tokens,
        grad_mask_token,
        grad_norm1_gain,
        grad_norm1_bias,
        grad_qkv,
        grad_qv_bias,
        grad_proj,
        grad_proj_bias,
        grad_scale_attn,
        grad_norm2_gain,
        grad_norm2_bias,
        grad_fc1,
        grad_fc1_bias,
        grad_fc2,
        grad_fc2_bias,
        grad_scale_mlp,
    )


def solution(mesh):
    return jax.shard_map(
        shards,
        mesh=mesh,
        in_specs=(
            P(("wide", "narrow"), None),
            P(("wide", "narrow")),
            P("wide"),
            P("wide"),
            P(),
            P(),
            P(),
            P(None, None, "narrow"),
            P(None, "narrow"),
            P("narrow", None),
            P(),
            P(),
            P(),
            P(),
            P(None, "narrow"),
            P("narrow"),
            P("narrow", None),
            P(),
            P(),
            P(("wide", "narrow"), None),
        ),
        out_specs=(
            P(("wide", "narrow"), None),
            P(("wide", "narrow"), None),
            P(),
            P(),
            P(),
            P(None, None, "narrow"),
            P(None, "narrow"),
            P("narrow", None),
            P(),
            P(),
            P(),
            P(),
            P(None, "narrow"),
            P("narrow"),
            P("narrow", None),
            P(),
            P(),
        ),
        check_vma=False,
    )
```

profile of v0, /device:TPU:0, one launch (start us, length us, event | category | flops | bytes accessed | tf_op | source)
XLA Modules:
  0.0 672.5 jit_solution(14743792329770781047)
XLA Ops:
  15.7 29.3 %all-gather.5.cloned.1.call-done = bf16[1024,768]{1,0:T(8,128)(2,1)} async-done(((bf16[512,768]{1,0:T(8,128)(2,1)}), bf16[1024,768]{1,0:T(8,128)(2,1)}) %all-gather.5.cloned.1.call-update) | async-done | bytes 1572880 | tf_op jit(solution)/shard_map/all_gather | solution.py:98
  45.0 4.0 convolution_bitcast_fusion
  50.9 29.5 %while.27 = (s32[]{:T(128)}, bf16[2,512,6,64]{1,3,2,0:T(8,128)(2,1)}, f32[2,6,512]{2,1,0:T(8,128)S(1)}, s32[2]{0:T(128)S(1)}, s32[1024]{0:T(1024)S(1)}, /*index=...) while((s32[]{:T(128)}, ...), condition=%wide.region_9.10_spmd, body=%wide.region_6.9_spmd.sunk | while | flops 846395392 | bytes 51779372 | solution.py:130
  53.3 3.4 fusion.120
  56.7 3.6 fusion.121
  60.4 4.4 fusion.122
  68.1 3.4 fusion.120
  71.5 3.6 fusion.121
  75.2 4.4 fusion.122
  80.5 2.0 copy.55
  83.6 2.2 convolution_convert_fusion
  86.2 25.7 %reduce-scatter.5.cloned.1.call-done = bf16[512,768]{1,0:T(8,128)(2,1)} async-done(((bf16[1024,768]{1,0:T(8,128)(2,1)}), bf16[512,768]{1,0:T(8,128)(2,1)}) %reduce-scatter.5.cloned.1.call-update) | async-done | bytes 786448 | tf_op jit(solution)/shard_map/reduce_scatter | solution.py:132
  112.0 2.0 fusion.60
  116.4 2.9 convert_reduce_fusion.3
  119.4 24.2 %all-gather.7.cloned.1.call-done = bf16[1024,768]{1,0:T(8,128)(2,1)} async-done(((bf16[512,768]{1,0:T(8,128)(2,1)}), bf16[1024,768]{1,0:T(8,128)(2,1)}) %all-gather.7.cloned.1.call-update) | async-done | bytes 1572880 | tf_op jit(solution)/shard_map/all_gather | solution.py:144
  143.6 7.4 %fusion.65 = f32[1024,1536]{1,0:T(8,128)} fusion(bf16[1024,768]{1,0:T(8,128)(2,1)} %all-gather.7.cloned.1.call-done, bf16[768,1536]{1,0:T(8,128)(2,1)} %param.38), kind=kOutput, calls=%fused_computation.152 | convolution fusion | flops 2415919104 | bytes 10223616 | tf_op jit(solution)/shard_map/dot_general | solution.py:145
  151.0 21.9 %all-gather.9.cloned.1.call-done = bf16[1024,768]{1,0:T(8,128)(2,1)} async-done(((bf16[512,768]{1,0:T(8,128)(2,1)}), bf16[1024,768]{1,0:T(8,128)(2,1)}) %all-gather.9.cloned.1.call-update) | async-done | bytes 1572880 | tf_op jit(solution)/shard_map/all_gather | solution.py:165
  172.9 20.0 %convert_reduce_fusion = (f32[1536]{0:T(1024)}, bf16[1024,1536]{1,0:T(8,128)(2,1)S(1)}, f32[1024,1536]{1,0:T(8,128)}) fusion(f32[1024,1536]{1,0:T(8,128)} %fusion.65, f32[1536]{0:T(1024)S(1)} %convert_element_type.194, bf16[1024,768]{1,0:T(8,128)(2,1)} %all-gather.9.cloned.1.call-done, bf16[1536,768]{1,0:T(8,128)(2,1)S(1)} %copy-done), kind=kOutput, calls=%fused_computation.49 | convolution fusion | flops 2533882368 | bytes 19673088 | tf_op jit(solution)/shard_map/rd,fd->rf/dot_general | solution.py:169
  194.5 3.7 convolution_convert_fusion.1
  198.3 6.2 multiply_convert_fusion.1
  206.2 3.7 convolution_convert_fusion.2
  209.9 14.5 %reduce-scatter.9.cloned.1.call-done = bf16[512,768]{1,0:T(8,128)(2,1)} async-done(((bf16[1024,768]{1,0:T(8,128)(2,1)}), bf16[512,768]{1,0:T(8,128)(2,1)}) %reduce-scatter.9.cloned.1.call-update) | async-done | bytes 786448 | tf_op jit(solution)/shard_map/reduce_scatter | solution.py:174
  224.5 2.7 convert_reduce_fusion.2
  229.0 24.3 %reduce-scatter.7.cloned.1.call-done = bf16[512,768]{1,0:T(8,128)(2,1)} async-done(((bf16[1024,768]{1,0:T(8,128)(2,1)}), bf16[512,768]{1,0:T(8,128)(2,1)}) %reduce-scatter.7.cloned.1.call-update) | async-done | bytes 786448 | tf_op jit(solution)/shard_map/reduce_scatter | solution.py:150
  253.3 4.2 multiply_reduce_fusion.2
  260.5 27.3 %all-gather.11.cloned.1.call-done = bf16[1024,768]{1,0:T(8,128)(2,1)} async-done(((bf16[512,768]{1,0:T(8,128)(2,1)}), bf16[1024,768]{1,0:T(8,128)(2,1)}) %all-gather.11.cloned.1.call-update) | async-done | bytes 1572880 | tf_op jit(solution)/shard_map/all_gather | solution.py:191
  287.7 3.3 convolution_convert_fusion.3
  291.1 56.1 %while.28 = (s32[]{:T(128)}, f32[1024,6,64]{0,2,1:T(8,128)S(1)}, f32[1024,6,64]{0,2,1:T(8,128)}, bf16[2,512,6,64]{1,3,2,0:T(8,128)(2,1)}, s32[2]{0:T(128)S(1)}, ...) while((s32[]{:T(128)}, f32[1024,6,64]{0,2,1:T(8,128)S(1)}, ...), condition=%wide.region_19.20_spmd.clone, body=%wide.region_17.19_spmd.clone.sunk | while | flops 2075195392 | bytes 132757464 | solution.py:239
  297.1 3.7 bitcast_add_fusion.5
  300.8 7.6 %multiply_reduce_fusion.6 = (f32[6,512]{1,0:T(8,128)S(1)}, f32[6,512,1024]{2,1,0:T(8,128)}) fusion(f32[6,512]{1,0:T(8,128)S(1)} %dynamic-slice_bitcast_fusion.2, f32[6,512,1024]{2,1,0:T(8,128)S(1)} %fusion.132, pred[512,1024]{1,0:T(8,128)(4,1)S(1)} %fusion.134, bf16[1024,6,64]{0,2,1:T(8,128)(2,1)S(1)} %copy-done.27, ...), kind=kOutput, calls=%fused_computation.20.clone.1 | convolution fusion | flops 421524480 | bytes 26898436 | tf_op jit(solution)/shard_map/while/body/eval_jaxpr/qhd,khd->hqk/dot_general | solution.py:220
  308.4 7.3 %multiply_convert_fusion.7 = bf16[6,512,1024]{2,1,0:T(8,128)(2,1)S(1)} fusion(f32[6,512,1024]{2,1,0:T(8,128)} %get-tuple-element.462, f32[6,512]{1,0:T(8,128)S(1)} %get-tuple-element.463, f32[6,512]{1,0:T(8,128)S(1)} %dynamic-slice_bitcast_fusion.2, f32[6,512,1024]{2,1,0:T(8,128)S(1)} %fusion.132, pred[512,1024]{1,0:T(8,128)(4,1)S(1)} %fusion.134), kind=kLoop, calls=%fused_computation.19.clone.1 | loop fusion | flops 22020096 | bytes 32006144 | tf_op jit(solution)/shard_map/while/body/eval_jaxpr/convert_element_type | solution.py:224
  315.6 2.0 fusion.135
  324.9 3.7 bitcast_add_fusion.5
  328.7 7.6 %multiply_reduce_fusion.6 = (f32[6,512]{1,0:T(8,128)S(1)}, f32[6,512,1024]{2,1,0:T(8,128)}) fusion(f32[6,512]{1,0:T(8,128)S(1)} %dynamic-slice_bitcast_fusion.2, f32[6,512,1024]{2,1,0:T(8,128)S(1)} %fusion.132, pred[512,1024]{1,0:T(8,128)(4,1)S(1)} %fusion.134, bf16[1024,6,64]{0,2,1:T(8,128)(2,1)S(1)} %copy-done.27, ...), kind=kOutput, calls=%fused_computation.20.clone.1 | convolution fusion | flops 421524480 | bytes 26898436 | tf_op jit(solution)/shard_map/while/body/eval_jaxpr/qhd,khd->hqk/dot_general | solution.py:220
  336.3 7.3 %multiply_convert_fusion.7 = bf16[6,512,1024]{2,1,0:T(8,128)(2,1)S(1)} fusion(f32[6,512,1024]{2,1,0:T(8,128)} %get-tuple-element.462, f32[6,512]{1,0:T(8,128)S(1)} %get-tuple-element.463, f32[6,512]{1,0:T(8,128)S(1)} %dynamic-slice_bitcast_fusion.2, f32[6,512,1024]{2,1,0:T(8,128)S(1)} %fusion.132, pred[512,1024]{1,0:T(8,128)(4,1)S(1)} %fusion.134), kind=kLoop, calls=%fused_computation.19.clone.1 | loop fusion | flops 22020096 | bytes 32006144 | tf_op jit(solution)/shard_map/while/body/eval_jaxpr/convert_element_type | solution.py:224
  343.5 2.0 fusion.135
  352.4 5.8 bitcast_convert_fusion
  358.2 5.9 fusion.68
  364.2 4.4 fusion.67
  371.1 3.9 convolution_bitcast_fusion.1
  376.5 64.4 %all-reduce.1 = (f32[2,384]{1,0:T(2,128)}, f32[1536]{0:T(1024)}) all-reduce(f32[2,384]{1,0:T(2,128)S(1)} %pad_maximum_fusion.3, f32[1536]{0:T(1024)S(1)} %copy-done.53), channel_id=1, replica_groups=mesh['wide'=16,'narrow'=2] {'wide'}, use_global_device_ids=true, to_apply=%region_32.33 | all-reduce | flops 2304 | bytes 18432 | tf_op jit(solution)/shard_map/psum | solution.py:254
  442.9 2.1 fusion.47
  447.0 39.9 %all-reduce = (f32[768]{0:T(1024)}, f32[768]{0:T(1024)}, f32[768]{0:T(1024)}, f32[768]{0:T(1024)}, f32[768]{0:T(1024)}, /*index=5*/f32[768]{0:T(1024)}, f32[768]{0:T(1024)}, f32[768]{0:T(1024)}, f32[768]{0:T(1024)}) all-reduce(f32[768]{0:T(1024)S(1)} %get-tuple-element.308, ...), channel_id=1, replica_groups=mesh['wide'=16,'narrow'=2] {'wide','narrow'}, use_global_device_ids=true, to_apply=%region_24.25 | all-reduce | flops 6912 | bytes 55296 | tf_op jit(solution)/shard_map/psum | solution.py:280
  486.9 2.8 broadcast_select_fusion
  489.7 160.6 %all-reduce.5.cloned.1.call-done = (f32[3,768,384]{1,2,0:T(8,128)}, f32[384,768]{1,0:T(8,128)}, f32[768,1536]{1,0:T(8,128)}, f32[1536,768]{1,0:T(8,128)}) async-done(((f32[3,768,384]{1,2,0:T(8,128)}, f32[384,768]{1,0:T(8,128)}, f32[768,1536]{1,0:T(8,128)}, f32[1536,768]{1,0:T(8,128)}), (f32[3,768,384]{1,2,0:T(8,128)}, f32[384,768]{1,0:T(8,128)}, f32[768,1536]{1,0:T(8,128)}, ...) | async-done | bytes 14155792 | tf_op jit(solution)/shard_map/psum | solution.py:254
  650.3 5.2 copy.61
  656.6 5.5 copy.94
  662.1 2.4 copy.95
  (273 shorter events, 52.3 us)
Async XLA Ops:
  7.2 165.7 %copy-start = (bf16[1536,768]{1,0:T(8,128)(2,1)S(1)}, bf16[1536,768]{1,0:T(8,128)(2,1)}, u32[]{:S(2)}) copy-start(bf16[1536,768]{1,0:T(8,128)(2,1)} %param.40) | copy-start | bytes 7077892
  7.2 6.2 copy-start.2
  7.2 37.8 %all-gather.5.cloned.1.call-start = ((), (), s32[]{:S(2)}) async-start(), calls=%async_computation.4 | async-start | bytes 2359296 | tf_op jit(solution)/shard_map/all_gather | solution.py:98
  8.1 245.1 %copy-start.39 = (pred[512]{0:T(512)(128)(4,1)}, pred[512]{0:T(512)(128)(4,1)S(1)}, u32[]{:S(2)}) copy-start(pred[512]{0:T(512)(128)(4,1)S(1)} %broadcast_compare_fusion) | copy-start | bytes 1540
  8.8 244.4 %copy-start.35 = (f32[768]{0:T(1024)}, f32[768]{0:T(1024)S(1)}, u32[]{:S(2)}) copy-start(f32[768]{0:T(1024)S(1)} %convert_element_type.177) | copy-start | bytes 9220
  10.3 4.7 copy-start.61
  10.3 4.9 copy-start.62
  10.3 4.9 copy-start.67
  10.4 5.3 copy-start.41
  12.0 37.1 %copy-start.43 = (f32[512]{0:T(512)}, f32[512]{0:T(512)S(1)}, u32[]{:S(2)}) copy-start(f32[512]{0:T(512)S(1)} %fusion.55) | copy-start | bytes 6148
  14.9 97.0 %reduce-scatter.5.cloned.1.call-start = ((), (), s32[]{:S(2)}) async-start(), calls=%async_computation.5 | async-start | bytes 2359296 | tf_op jit(solution)/shard_map/reduce_scatter | solution.py:132
  56.7 3.7 copy-start.26
  71.5 3.7 copy-start.26
  85.7 57.8 %all-gather.7.cloned.1.call-start = ((), (), s32[]{:S(2)}) async-start(), calls=%async_computation.6 | async-start | bytes 2359296 | tf_op jit(solution)/shard_map/all_gather | solution.py:144
  116.2 56.7 %all-gather.9.cloned.1.call-start = ((), (), s32[]{:S(2)}) async-start(), calls=%async_computation.8 | async-start | bytes 2359296 | tf_op jit(solution)/shard_map/all_gather | solution.py:165
  119.3 105.2 %reduce-scatter.9.cloned.1.call-start = ((), (), s32[]{:S(2)}) async-start(), calls=%async_computation.9 | async-start | bytes 2359296 | tf_op jit(solution)/shard_map/reduce_scatter | solution.py:174
  172.9 21.6 %copy-start.63 = (bf16[768,1536]{1,0:T(8,128)(2,1)S(1)}, bf16[768,1536]{1,0:T(8,128)(2,1)}, u32[]{:S(2)}) copy-start(bf16[768,1536]{1,0:T(8,128)(2,1)} %param.38) | copy-start | bytes 7077892
  198.2 55.0 %reduce-scatter.7.cloned.1.call-start = ((), (), s32[]{:S(2)}) async-start(), calls=%async_computation.7 | async-start | bytes 2359296 | tf_op jit(solution)/shard_map/reduce_scatter | solution.py:150
  206.2 3.7 copy-start.60
  209.8 14.6 %copy-start.4 = (bf16[512,768]{1,0:T(8,128)(2,1)S(1)}, bf16[512,768]{1,0:T(8,128)(2,1)}, u32[]{:S(2)}) copy-start(bf16[512,768]{1,0:T(8,128)(2,1)} %param.24) | copy-start | bytes 2359300
  209.8 14.6 %copy-start.8 = (bf16[512,768]{1,0:T(8,128)(2,1)S(1)}, bf16[512,768]{1,0:T(8,128)(2,1)}, u32[]{:S(2)}) copy-start(bf16[512,768]{1,0:T(8,128)(2,1)} %reduce-scatter.5.cloned.1.call-done) | copy-start | bytes 2359300
  209.9 77.9 %all-gather.11.cloned.1.call-start = ((), (), s32[]{:S(2)}) async-start(), calls=%async_computation.10 | async-start | bytes 2359296 | tf_op jit(solution)/shard_map/all_gather | solution.py:191
  260.4 180.6 %reduce-scatter.11.cloned.1.call-start = ((), (), s32[]{:S(2)}) async-start(), calls=%async_computation.11 | async-start | bytes 2359296 | tf_op jit(solution)/shard_map/reduce_scatter | solution.py:257
  260.4 30.6 %copy-start.6 = (bf16[1024,6,64]{0,2,1:T(8,128)(2,1)S(1)}, bf16[1024,6,64]{0,2,1:T(8,128)(2,1)}, u32[]{:S(2)}) copy-start(bf16[1024,6,64]{0,2,1:T(8,128)(2,1)} %get-tuple-element.588) | copy-start | bytes 2359300
  297.1 3.7 copy-start.27
  300.8 7.6 %copy-start.23 = (f32[1024,6,64]{0,2,1:T(8,128)}, f32[1024,6,64]{0,2,1:T(8,128)S(1)}, u32[]{:S(2)}) copy-start(f32[1024,6,64]{0,2,1:T(8,128)S(1)} %bitcast_add_fusion.5) | copy-start | bytes 4718596 | tf_op jit(solution)/shard_map/while
  308.4 7.3 %copy-start.15 = (bf16[2,512,6,64]{1,3,2,0:T(8,128)(2,1)S(1)}, bf16[2,512,6,64]{1,3,2,0:T(8,128)(2,1)}, u32[]{:S(2)}) copy-start(bf16[2,512,6,64]{1,3,2,0:T(8,128)(2,1)} %get-tuple-element.523) | copy-start | bytes 2359300 | tf_op jit(solution)/shard_map/while
  324.9 3.7 copy-start.27
  328.6 7.6 %copy-start.23 = (f32[1024,6,64]{0,2,1:T(8,128)}, f32[1024,6,64]{0,2,1:T(8,128)S(1)}, u32[]{:S(2)}) copy-start(f32[1024,6,64]{0,2,1:T(8,128)S(1)} %bitcast_add_fusion.5) | copy-start | bytes 4718596 | tf_op jit(solution)/shard_map/while
  336.3 7.3 %copy-start.15 = (bf16[2,512,6,64]{1,3,2,0:T(8,128)(2,1)S(1)}, bf16[2,512,6,64]{1,3,2,0:T(8,128)(2,1)}, u32[]{:S(2)}) copy-start(bf16[2,512,6,64]{1,3,2,0:T(8,128)(2,1)} %get-tuple-element.523) | copy-start | bytes 2359300 | tf_op jit(solution)/shard_map/while
  352.4 5.8 copy-start.14
  358.2 292.2 %all-reduce.5.cloned.1.call-start = ((), (), s32[]{:S(2)}) async-start(), calls=%async_computation.12 | async-start | bytes 28311552 | tf_op jit(solution)/shard_map/psum | solution.py:254
  358.2 5.9 copy-start.20
  358.2 5.9 copy-start.21
  364.1 4.4 copy-start.29
  364.1 4.4 copy-start.65
  375.0 65.9 %copy-start.5 = (bf16[512,768]{1,0:T(8,128)(2,1)S(1)}, bf16[512,768]{1,0:T(8,128)(2,1)}, u32[]{:S(2)}) copy-start(bf16[512,768]{1,0:T(8,128)(2,1)} %param.24) | copy-start | bytes 2359300
  375.0 65.9 %copy-start.36 = (f32[768]{0:T(1024)S(1)}, f32[768]{0:T(1024)}, u32[]{:S(2)}) copy-start(f32[768]{0:T(1024)} %copy-done.35) | copy-start | bytes 9220
  375.0 65.9 %copy-start.38 = (f32[768]{0:T(1024)S(1)}, f32[768]{0:T(1024)}, u32[]{:S(2)}) copy-start(f32[768]{0:T(1024)} %copy-done.37) | copy-start | bytes 9220
  375.0 65.9 %copy-start.40 = (pred[512]{0:T(512)(128)(4,1)S(1)}, pred[512]{0:T(512)(128)(4,1)}, u32[]{:S(2)}) copy-start(pred[512]{0:T(512)(128)(4,1)} %copy-done.39) | copy-start | bytes 1540
  375.0 65.9 %copy-start.42 = (f32[512]{0:T(512)S(1)}, f32[512]{0:T(512)}, u32[]{:S(2)}) copy-start(f32[512]{0:T(512)} %copy-done.41) | copy-start | bytes 6148
  376.1 66.8 %copy-start.46 = (f32[512]{0:T(512)S(1)}, f32[512]{0:T(512)}, u32[]{:S(2)}) copy-start(f32[512]{0:T(512)} %copy-done.45) | copy-start | bytes 6148
  376.1 66.8 %copy-start.44 = (f32[512]{0:T(512)S(1)}, f32[512]{0:T(512)}, u32[]{:S(2)}) copy-start(f32[512]{0:T(512)} %copy-done.43) | copy-start | bytes 6148
  376.3 68.7 %copy-start.10 = (f32[512,768]{1,0:T(8,128)S(1)}, f32[512,768]{1,0:T(8,128)}, u32[]{:S(2)}) copy-start(f32[512,768]{1,0:T(8,128)} %copy-done.9) | copy-start | bytes 4718596
  441.0 4.1 copy-start.11
  650.3 5.3 copy-start.25
  655.6 6.5 slice-start
  656.6 5.5 slice-start.1
  (41 other events, 81.7 us)
Sparse Core Ops, SparseCore 0:
  15.1 29.8 all-gather.4
  85.9 26.0 reduce-scatter.4
  116.3 27.2 all-gather.6
  145.6 27.2 all-gather.8
  198.4 26.0 reduce-scatter.8
  227.2 26.0 reduce-scatter.6
  260.5 27.2 all-gather.10
  358.3 26.0 reduce-scatter.10
  390.1 260.1 all-reduce.4
where the time goes:
time: 681 us; the launch traced here: 672 us
  waiting for transfers between devices  328 us (48%)
  matrix products  115 us (17%)
  blocking collectives  104 us (15%)
  other arithmetic  68.1 us (10%)
  local copies, waits for them, and re-layouts  34.9 us (5%)
  between operations  15 us (2%)
    psum x1, waiting for transfers between devices, shards(): lax.psum((grad_qkv, grad_qv_bias, grad_proj, grad_fc1, grad_fc1_bias, gra...  161 us
    psum x1, blocking collectives, shards(): lax.psum((grad_qkv, grad_qv_bias, grad_proj, grad_fc1, grad_fc1_bias, gra...  64.4 us
    psum x1, blocking collectives, shards(): lax.psum((grad_mask_token, grad_norm1_gain, grad_norm1_bias, grad_proj_bi...  39.9 us
    all_gather x1, waiting for transfers between devices, shards(): normed1_all = lax.all_gather(normed1, 'narrow', axis=0, tiled=True)  29.3 us
    all_gather x1, waiting for transfers between devices, shards(): grad_attn_all = lax.all_gather(grad_attn, 'narrow', axis=0, tiled=True)  27.3 us
    reduce_scatter x1, waiting for transfers between devices, shards(): lax.psum_scatter(jnp.dot(slab(heads_out, jnp.int32(0), own_rows * lax.axi...  25.7 us
    reduce_scatter x1, waiting for transfers between devices, shards(): lax.psum_scatter(jnp.dot(slab(activated, jnp.int32(0), own_rows * lax.axi...  24.3 us
    all_gather x1, waiting for transfers between devices, shards(): normed2_all = lax.all_gather(normed2, 'narrow', axis=0, tiled=True)  24.2 us
  transfers between devices with their start and end apart: 9, of which 8 were waited for; matrix products, arithmetic and copies ran while one was open for 7% of the time, Pallas kernels for 0%

commit v1 on v0

--- a/solution.py
+++ b/solution.py
@@ -12,6 +12,11 @@
 epsilon = 1e-06
 score_scale = 0.125
 masked_score = -1e30
+
+
+def axis_by_axis(x, one, other):
+    inner = lax.psum(x, one)
+    return lax.psum(inner, other)
 
 
 def layer_norm(values_in, norm_gain, norm_shift):
@@ -277,7 +282,7 @@
         grad_norm2_bias,
         grad_fc2_bias,
         grad_scale_mlp,
-    ) = lax.psum(
+    ) = axis_by_axis(
         (
             grad_mask_token,
             grad_norm1_gain,
@@ -289,7 +294,8 @@
             grad_fc2_bias,
             grad_scale_mlp,
         ),
-        ("wide", "narrow"),
+        "narrow",
+        "wide",
     )
     return (
         output,

time: 681 us -> 681 us (level)
  blocking collectives: 104 us -> 71.4 us
  waiting for transfers between devices: 328 us -> 360 us
    psum x2, blocking collectives: 104 us -> 71.4 us  [the longest x1 64.1 us: axis_by_axis(): return lax.psum(inner, other)]
    psum x1, waiting for transfers between devices: 161 us -> 185 us  [shards(): lax.psum((grad_qkv, grad_qv_bias, grad_proj, grad_fc1, grad_fc1_bias, gra...]
    reduce_scatter x1, waiting for transfers between devices: 0.01 us -> 7.88 us  [shards(): lax.psum_scatter(jnp.einsum('cre,cde->rd', grad_stack, w_qkv, preferred_e...]
  transfers between devices with their start and end apart: 9 -> 9, of which waited for: 8 -> 9; matrix products, arithmetic and copies ran while one was open for 7% -> 7% of each run, Pallas kernels for 0% -> 0%
where the time goes in v1:
time: 681 us; the launch traced here: 672 us
  waiting for transfers between devices  360 us (53%)
  matrix products  114 us (17%)
  blocking collectives  71.4 us (10%)
  other arithmetic  68 us (10%)
  local copies, waits for them, and re-layouts  35 us (5%)
  between operations  15 us (2%)
  loops' own time  7.12 us (1%)
    psum x1, waiting for transfers between devices, shards(): lax.psum((grad_qkv, grad_qv_bias, grad_proj, grad_fc1, grad_fc1_bias, gra...  185 us
    psum x1, blocking collectives, axis_by_axis(): return lax.psum(inner, other)  64.1 us
    all_gather x1, waiting for transfers between devices, shards(): normed1_all = lax.all_gather(normed1, 'narrow', axis=0, tiled=True)  29.3 us
    all_gather x1, waiting for transfers between devices, shards(): grad_attn_all = lax.all_gather(grad_attn, 'narrow', axis=0, tiled=True)  27.3 us
    reduce_scatter x1, waiting for transfers between devices, shards(): lax.psum_scatter(jnp.dot(slab(heads_out, jnp.int32(0), own_rows * lax.axi...  25.8 us
    reduce_scatter x1, waiting for transfers between devices, shards(): lax.psum_scatter(jnp.dot(slab(activated, jnp.int32(0), own_rows * lax.axi...  24.3 us
    all_gather x1, waiting for transfers between devices, shards(): normed2_all = lax.all_gather(normed2, 'narrow', axis=0, tiled=True)  24.2 us
    unnamed x129, local copies, waits for them, and re-layouts  22.7 us
  transfers between devices with their start and end apart: 9, of which 9 were waited for; matrix products, arithmetic and copies ran while one was open for 7% of the time, Pallas kernels for 0%

profile of v1, /device:TPU:0, one launch (start us, length us, event | category | flops | bytes accessed | tf_op | source)
XLA Modules:
  0.0 671.9 jit_solution(10740765388859022304)
XLA Ops:
  15.7 29.3 %all-gather.5.cloned.1.call-done = bf16[1024,768]{1,0:T(8,128)(2,1)} async-done(((bf16[512,768]{1,0:T(8,128)(2,1)}), bf16[1024,768]{1,0:T(8,128)(2,1)}) %all-gather.5.cloned.1.call-update) | async-done | bytes 1572880 | tf_op jit(solution)/shard_map/all_gather | solution.py:103
  45.0 4.0 convolution_bitcast_fusion
  51.0 29.5 %while.27 = (s32[]{:T(128)}, bf16[2,512,6,64]{1,3,2,0:T(8,128)(2,1)}, f32[2,6,512]{2,1,0:T(8,128)S(1)}, s32[2]{0:T(128)S(1)}, s32[1024]{0:T(1024)S(1)}, /*index=...) while((s32[]{:T(128)}, ...), condition=%wide.region_9.10_spmd, body=%wide.region_6.9_spmd.sunk | while | flops 846395392 | bytes 51779372 | solution.py:135
  53.3 3.4 fusion.120
  56.7 3.6 fusion.121
  60.4 4.4 fusion.122
  68.1 3.4 fusion.120
  71.5 3.6 fusion.121
  75.2 4.4 fusion.122
  80.5 2.0 copy.55
  83.5 2.2 convolution_convert_fusion
  86.2 25.8 %reduce-scatter.5.cloned.1.call-done = bf16[512,768]{1,0:T(8,128)(2,1)} async-done(((bf16[1024,768]{1,0:T(8,128)(2,1)}), bf16[512,768]{1,0:T(8,128)(2,1)}) %reduce-scatter.5.cloned.1.call-update) | async-done | bytes 786448 | tf_op jit(solution)/shard_map/reduce_scatter | solution.py:137
  116.4 2.9 convert_reduce_fusion.3
  119.4 24.2 %all-gather.7.cloned.1.call-done = bf16[1024,768]{1,0:T(8,128)(2,1)} async-done(((bf16[512,768]{1,0:T(8,128)(2,1)}), bf16[1024,768]{1,0:T(8,128)(2,1)}) %all-gather.7.cloned.1.call-update) | async-done | bytes 1572880 | tf_op jit(solution)/shard_map/all_gather | solution.py:149
  143.6 7.4 %fusion.65 = f32[1024,1536]{1,0:T(8,128)} fusion(bf16[1024,768]{1,0:T(8,128)(2,1)} %all-gather.7.cloned.1.call-done, bf16[768,1536]{1,0:T(8,128)(2,1)} %param.38), kind=kOutput, calls=%fused_computation.152 | convolution fusion | flops 2415919104 | bytes 10223616 | tf_op jit(solution)/shard_map/dot_general | solution.py:150
  151.0 21.9 %all-gather.9.cloned.1.call-done = bf16[1024,768]{1,0:T(8,128)(2,1)} async-done(((bf16[512,768]{1,0:T(8,128)(2,1)}), bf16[1024,768]{1,0:T(8,128)(2,1)}) %all-gather.9.cloned.1.call-update) | async-done | bytes 1572880 | tf_op jit(solution)/shard_map/all_gather | solution.py:170
  172.9 20.0 %convert_reduce_fusion = (f32[1536]{0:T(1024)}, bf16[1024,1536]{1,0:T(8,128)(2,1)S(1)}, f32[1024,1536]{1,0:T(8,128)}) fusion(f32[1024,1536]{1,0:T(8,128)} %fusion.65, f32[1536]{0:T(1024)S(1)} %convert_element_type.194, bf16[1024,768]{1,0:T(8,128)(2,1)} %all-gather.9.cloned.1.call-done, bf16[1536,768]{1,0:T(8,128)(2,1)S(1)} %copy-done), kind=kOutput, calls=%fused_computation.49 | convolution fusion | flops 2533882368 | bytes 19673088 | tf_op jit(solution)/shard_map/rd,fd->rf/dot_general | solution.py:174
  194.5 3.7 convolution_convert_fusion.1
  198.3 6.2 multiply_convert_fusion.1
  206.2 3.7 convolution_convert_fusion.2
  209.9 14.5 %reduce-scatter.9.cloned.1.call-done = bf16[512,768]{1,0:T(8,128)(2,1)} async-done(((bf16[1024,768]{1,0:T(8,128)(2,1)}), bf16[512,768]{1,0:T(8,128)(2,1)}) %reduce-scatter.9.cloned.1.call-update) | async-done | bytes 786448 | tf_op jit(solution)/shard_map/reduce_scatter | solution.py:179
  224.5 2.7 convert_reduce_fusion.2
  228.9 24.3 %reduce-scatter.7.cloned.1.call-done = bf16[512,768]{1,0:T(8,128)(2,1)} async-done(((bf16[1024,768]{1,0:T(8,128)(2,1)}), bf16[512,768]{1,0:T(8,128)(2,1)}) %reduce-scatter.7.cloned.1.call-update) | async-done | bytes 786448 | tf_op jit(solution)/shard_map/reduce_scatter | solution.py:155
  253.3 4.2 multiply_reduce_fusion.2
  260.4 27.3 %all-gather.11.cloned.1.call-done = bf16[1024,768]{1,0:T(8,128)(2,1)} async-done(((bf16[512,768]{1,0:T(8,128)(2,1)}), bf16[1024,768]{1,0:T(8,128)(2,1)}) %all-gather.11.cloned.1.call-update) | async-done | bytes 1572880 | tf_op jit(solution)/shard_map/all_gather | solution.py:196
  287.7 3.3 convolution_convert_fusion.3
  291.0 56.5 %while.28 = (s32[]{:T(128)}, f32[1024,6,64]{0,2,1:T(8,128)S(1)}, f32[1024,6,64]{0,2,1:T(8,128)}, bf16[2,512,6,64]{1,3,2,0:T(8,128)(2,1)}, s32[2]{0:T(128)S(1)}, ...) while((s32[]{:T(128)}, f32[1024,6,64]{0,2,1:T(8,128)S(1)}, ...), condition=%wide.region_19.20_spmd.clone, body=%wide.region_17.19_spmd.clone.sunk | while | flops 2075195392 | bytes 132757464 | solution.py:244
  297.4 3.7 bitcast_add_fusion.5
  301.1 7.5 %multiply_reduce_fusion.6 = (f32[6,512]{1,0:T(8,128)S(1)}, f32[6,512,1024]{2,1,0:T(8,128)}) fusion(f32[6,512]{1,0:T(8,128)S(1)} %dynamic-slice_bitcast_fusion.2, f32[6,512,1024]{2,1,0:T(8,128)S(1)} %fusion.132, pred[512,1024]{1,0:T(8,128)(4,1)S(1)} %fusion.134, bf16[1024,6,64]{0,2,1:T(8,128)(2,1)S(1)} %copy-done.27, ...), kind=kOutput, calls=%fused_computation.20.clone.1 | convolution fusion | flops 421524480 | bytes 26898436 | tf_op jit(solution)/shard_map/while/body/eval_jaxpr/qhd,khd->hqk/dot_general | solution.py:225
  308.5 7.3 %multiply_convert_fusion.7 = bf16[6,512,1024]{2,1,0:T(8,128)(2,1)S(1)} fusion(f32[6,512,1024]{2,1,0:T(8,128)} %get-tuple-element.471, f32[6,512]{1,0:T(8,128)S(1)} %get-tuple-element.472, f32[6,512]{1,0:T(8,128)S(1)} %dynamic-slice_bitcast_fusion.2, f32[6,512,1024]{2,1,0:T(8,128)S(1)} %fusion.132, pred[512,1024]{1,0:T(8,128)(4,1)S(1)} %fusion.134), kind=kLoop, calls=%fused_computation.19.clone.1 | loop fusion | flops 22020096 | bytes 32006144 | tf_op jit(solution)/shard_map/while/body/eval_jaxpr/convert_element_type | solution.py:229
  315.8 2.0 fusion.135
  325.4 3.7 bitcast_add_fusion.5
  329.2 7.5 %multiply_reduce_fusion.6 = (f32[6,512]{1,0:T(8,128)S(1)}, f32[6,512,1024]{2,1,0:T(8,128)}) fusion(f32[6,512]{1,0:T(8,128)S(1)} %dynamic-slice_bitcast_fusion.2, f32[6,512,1024]{2,1,0:T(8,128)S(1)} %fusion.132, pred[512,1024]{1,0:T(8,128)(4,1)S(1)} %fusion.134, bf16[1024,6,64]{0,2,1:T(8,128)(2,1)S(1)} %copy-done.27, ...), kind=kOutput, calls=%fused_computation.20.clone.1 | convolution fusion | flops 421524480 | bytes 26898436 | tf_op jit(solution)/shard_map/while/body/eval_jaxpr/qhd,khd->hqk/dot_general | solution.py:225
  336.6 7.3 %multiply_convert_fusion.7 = bf16[6,512,1024]{2,1,0:T(8,128)(2,1)S(1)} fusion(f32[6,512,1024]{2,1,0:T(8,128)} %get-tuple-element.471, f32[6,512]{1,0:T(8,128)S(1)} %get-tuple-element.472, f32[6,512]{1,0:T(8,128)S(1)} %dynamic-slice_bitcast_fusion.2, f32[6,512,1024]{2,1,0:T(8,128)S(1)} %fusion.132, pred[512,1024]{1,0:T(8,128)(4,1)S(1)} %fusion.134), kind=kLoop, calls=%fused_computation.19.clone.1 | loop fusion | flops 22020096 | bytes 32006144 | tf_op jit(solution)/shard_map/while/body/eval_jaxpr/convert_element_type | solution.py:229
  343.9 2.0 fusion.135
  352.7 5.8 bitcast_convert_fusion
  358.6 5.9 fusion.68
  364.5 4.4 fusion.67
  371.5 3.9 convolution_bitcast_fusion.1
  376.9 7.9 %reduce-scatter.11.cloned.1.call-done = bf16[512,768]{1,0:T(8,128)(2,1)} async-done(((bf16[1024,768]{1,0:T(8,128)(2,1)}), bf16[512,768]{1,0:T(8,128)(2,1)}) %reduce-scatter.11.cloned.1.call-update) | async-done | bytes 786448 | tf_op jit(solution)/shard_map/reduce_scatter | solution.py:262
  386.8 2.1 fusion.47
  390.8 7.3 %all-reduce.2 = (f32[768]{0:T(1024)S(1)}, f32[768]{0:T(1024)S(1)}, f32[768]{0:T(1024)S(1)}, f32[768]{0:T(1024)S(1)}, f32[768]{0:T(1024)S(1)}, /*index=5*/f32[768...) all-reduce(f32[768]{0:T(1024)S(1)} %get-tuple-element.317, ...), channel_id=1, replica_groups=mesh['wide'=16,'narrow'=2] {'narrow'}, use_global_device_ids=true, to_apply=%region_24.25 | all-reduce | flops 6912 | bytes 55296 | tf_op jit(solution)/shard_map/psum | solution.py:18
  398.2 64.1 %all-reduce = (f32[768]{0:T(1024)}, f32[768]{0:T(1024)}, f32[768]{0:T(1024)}, f32[2,384]{1,0:T(2,128)}, f32[768]{0:T(1024)}, /*index=5*/f32[768]{0:T(1024)}, f32...) all-reduce(f32[768]{0:T(1024)S(1)} %get-tuple-element.293, ...), channel_id=1, replica_groups=mesh['wide'=16,'narrow'=2] {'wide'}, use_global_device_ids=true, to_apply=%region_25.26 | all-reduce | flops 9216 | bytes 73728 | tf_op jit(solution)/shard_map/psum | solution.py:19
  462.2 2.7 broadcast_select_fusion
  465.0 184.9 %all-reduce.5.cloned.1.call-done = (f32[3,768,384]{1,2,0:T(8,128)}, f32[384,768]{1,0:T(8,128)}, f32[768,1536]{1,0:T(8,128)}, f32[1536,768]{1,0:T(8,128)}) async-done(((f32[3,768,384]{1,2,0:T(8,128)}, f32[384,768]{1,0:T(8,128)}, f32[768,1536]{1,0:T(8,128)}, f32[1536,768]{1,0:T(8,128)}), (f32[3,768,384]{1,2,0:T(8,128)}, f32[384,768]{1,0:T(8,128)}, f32[768,1536]{1,0:T(8,128)}, ...) | async-done | bytes 14155792 | tf_op jit(solution)/shard_map/psum | solution.py:259
  649.9 5.2 copy.61
  656.1 5.5 copy.94
  661.7 2.4 copy.95
  (273 shorter events, 54.4 us)
Async XLA Ops:
  7.2 165.7 %copy-start = (bf16[1536,768]{1,0:T(8,128)(2,1)S(1)}, bf16[1536,768]{1,0:T(8,128)(2,1)}, u32[]{:S(2)}) copy-start(bf16[1536,768]{1,0:T(8,128)(2,1)} %param.40) | copy-start | bytes 7077892
  7.2 6.2 copy-start.2
  7.2 37.8 %all-gather.5.cloned.1.call-start = ((), (), s32[]{:S(2)}) async-start(), calls=%async_computation.4 | async-start | bytes 2359296 | tf_op jit(solution)/shard_map/all_gather | solution.py:103
  8.1 245.1 %copy-start.39 = (pred[512]{0:T(512)(128)(4,1)}, pred[512]{0:T(512)(128)(4,1)S(1)}, u32[]{:S(2)}) copy-start(pred[512]{0:T(512)(128)(4,1)S(1)} %broadcast_compare_fusion) | copy-start | bytes 1540
  8.9 244.4 %copy-start.35 = (f32[768]{0:T(1024)}, f32[768]{0:T(1024)S(1)}, u32[]{:S(2)}) copy-start(f32[768]{0:T(1024)S(1)} %convert_element_type.177) | copy-start | bytes 9220
  10.3 4.7 copy-start.61
  10.3 4.9 copy-start.62
  10.3 4.9 copy-start.67
  10.4 5.3 copy-start.41
  12.0 37.1 %copy-start.43 = (f32[512]{0:T(512)}, f32[512]{0:T(512)S(1)}, u32[]{:S(2)}) copy-start(f32[512]{0:T(512)S(1)} %fusion.55) | copy-start | bytes 6148
  15.0 97.0 %reduce-scatter.5.cloned.1.call-start = ((), (), s32[]{:S(2)}) async-start(), calls=%async_computation.5 | async-start | bytes 2359296 | tf_op jit(solution)/shard_map/reduce_scatter | solution.py:137
  56.7 3.7 copy-start.26
  85.7 57.9 %all-gather.7.cloned.1.call-start = ((), (), s32[]{:S(2)}) async-start(), calls=%async_computation.6 | async-start | bytes 2359296 | tf_op jit(solution)/shard_map/all_gather | solution.py:149
  116.2 56.7 %all-gather.9.cloned.1.call-start = ((), (), s32[]{:S(2)}) async-start(), calls=%async_computation.8 | async-start | bytes 2359296 | tf_op jit(solution)/shard_map/all_gather | solution.py:170
  119.3 105.2 %reduce-scatter.9.cloned.1.call-start = ((), (), s32[]{:S(2)}) async-start(), calls=%async_computation.9 | async-start | bytes 2359296 | tf_op jit(solution)/shard_map/reduce_scatter | solution.py:179
  172.9 21.6 %copy-start.63 = (bf16[768,1536]{1,0:T(8,128)(2,1)S(1)}, bf16[768,1536]{1,0:T(8,128)(2,1)}, u32[]{:S(2)}) copy-start(bf16[768,1536]{1,0:T(8,128)(2,1)} %param.38) | copy-start | bytes 7077892
  198.3 55.0 %reduce-scatter.7.cloned.1.call-start = ((), (), s32[]{:S(2)}) async-start(), calls=%async_computation.7 | async-start | bytes 2359296 | tf_op jit(solution)/shard_map/reduce_scatter | solution.py:155
  206.2 3.7 copy-start.60
  209.8 14.6 %copy-start.4 = (bf16[512,768]{1,0:T(8,128)(2,1)S(1)}, bf16[512,768]{1,0:T(8,128)(2,1)}, u32[]{:S(2)}) copy-start(bf16[512,768]{1,0:T(8,128)(2,1)} %param.24) | copy-start | bytes 2359300
  209.8 14.6 %copy-start.8 = (bf16[512,768]{1,0:T(8,128)(2,1)S(1)}, bf16[512,768]{1,0:T(8,128)(2,1)}, u32[]{:S(2)}) copy-start(bf16[512,768]{1,0:T(8,128)(2,1)} %reduce-scatter.5.cloned.1.call-done) | copy-start | bytes 2359300
  209.9 77.8 %all-gather.11.cloned.1.call-start = ((), (), s32[]{:S(2)}) async-start(), calls=%async_computation.10 | async-start | bytes 2359296 | tf_op jit(solution)/shard_map/all_gather | solution.py:196
  260.3 124.4 %reduce-scatter.11.cloned.1.call-start = ((), (), s32[]{:S(2)}) async-start(), calls=%async_computation.11 | async-start | bytes 2359296 | tf_op jit(solution)/shard_map/reduce_scatter | solution.py:262
  260.4 30.6 %copy-start.6 = (bf16[1024,6,64]{0,2,1:T(8,128)(2,1)S(1)}, bf16[1024,6,64]{0,2,1:T(8,128)(2,1)}, u32[]{:S(2)}) copy-start(bf16[1024,6,64]{0,2,1:T(8,128)(2,1)} %get-tuple-element.597) | copy-start | bytes 2359300
  297.4 3.7 copy-start.27
  301.0 7.5 %copy-start.23 = (f32[1024,6,64]{0,2,1:T(8,128)}, f32[1024,6,64]{0,2,1:T(8,128)S(1)}, u32[]{:S(2)}) copy-start(f32[1024,6,64]{0,2,1:T(8,128)S(1)} %bitcast_add_fusion.5) | copy-start | bytes 4718596 | tf_op jit(solution)/shard_map/while
  308.5 7.3 %copy-start.15 = (bf16[2,512,6,64]{1,3,2,0:T(8,128)(2,1)S(1)}, bf16[2,512,6,64]{1,3,2,0:T(8,128)(2,1)}, u32[]{:S(2)}) copy-start(bf16[2,512,6,64]{1,3,2,0:T(8,128)(2,1)} %get-tuple-element.532) | copy-start | bytes 2359300 | tf_op jit(solution)/shard_map/while
  325.4 3.7 copy-start.27
  329.1 7.5 %copy-start.23 = (f32[1024,6,64]{0,2,1:T(8,128)}, f32[1024,6,64]{0,2,1:T(8,128)S(1)}, u32[]{:S(2)}) copy-start(f32[1024,6,64]{0,2,1:T(8,128)S(1)} %bitcast_add_fusion.5) | copy-start | bytes 4718596 | tf_op jit(solution)/shard_map/while
  336.6 7.3 %copy-start.15 = (bf16[2,512,6,64]{1,3,2,0:T(8,128)(2,1)S(1)}, bf16[2,512,6,64]{1,3,2,0:T(8,128)(2,1)}, u32[]{:S(2)}) copy-start(bf16[2,512,6,64]{1,3,2,0:T(8,128)(2,1)} %get-tuple-element.532) | copy-start | bytes 2359300 | tf_op jit(solution)/shard_map/while
  352.7 5.9 copy-start.14
  358.5 291.3 %all-reduce.5.cloned.1.call-start = ((), (), s32[]{:S(2)}) async-start(), calls=%async_computation.12 | async-start | bytes 28311552 | tf_op jit(solution)/shard_map/psum | solution.py:259
  358.6 5.9 copy-start.20
  358.6 5.9 copy-start.21
  364.5 4.4 copy-start.29
  364.5 4.4 copy-start.65
  375.4 9.4 %copy-start.5 = (bf16[512,768]{1,0:T(8,128)(2,1)S(1)}, bf16[512,768]{1,0:T(8,128)(2,1)}, u32[]{:S(2)}) copy-start(bf16[512,768]{1,0:T(8,128)(2,1)} %param.24) | copy-start | bytes 2359300
  375.4 9.4 %copy-start.36 = (f32[768]{0:T(1024)S(1)}, f32[768]{0:T(1024)}, u32[]{:S(2)}) copy-start(f32[768]{0:T(1024)} %copy-done.35) | copy-start | bytes 9220
  375.4 9.4 %copy-start.38 = (f32[768]{0:T(1024)S(1)}, f32[768]{0:T(1024)}, u32[]{:S(2)}) copy-start(f32[768]{0:T(1024)} %copy-done.37) | copy-start | bytes 9220
  375.4 9.4 %copy-start.40 = (pred[512]{0:T(512)(128)(4,1)S(1)}, pred[512]{0:T(512)(128)(4,1)}, u32[]{:S(2)}) copy-start(pred[512]{0:T(512)(128)(4,1)} %copy-done.39) | copy-start | bytes 1540
  375.4 9.4 %copy-start.42 = (f32[512]{0:T(512)S(1)}, f32[512]{0:T(512)}, u32[]{:S(2)}) copy-start(f32[512]{0:T(512)} %copy-done.41) | copy-start | bytes 6148
  376.5 10.2 %copy-start.46 = (f32[512]{0:T(512)S(1)}, f32[512]{0:T(512)}, u32[]{:S(2)}) copy-start(f32[512]{0:T(512)} %copy-done.45) | copy-start | bytes 6148
  376.5 10.2 %copy-start.44 = (f32[512]{0:T(512)S(1)}, f32[512]{0:T(512)}, u32[]{:S(2)}) copy-start(f32[512]{0:T(512)} %copy-done.43) | copy-start | bytes 6148
  376.7 12.2 %copy-start.10 = (f32[512,768]{1,0:T(8,128)S(1)}, f32[512,768]{1,0:T(8,128)}, u32[]{:S(2)}) copy-start(f32[512,768]{1,0:T(8,128)} %copy-done.9) | copy-start | bytes 4718596
  384.8 4.1 copy-start.11
  389.0 9.2 %copy-start.53 = (f32[1536]{0:T(1024)S(1)}, f32[1536]{0:T(1024)}, u32[]{:S(2)}) copy-start(f32[1536]{0:T(1024)} %get-tuple-element.306) | copy-start | bytes 18436
  649.9 5.3 copy-start.25
  655.1 6.5 slice-start
  656.1 5.5 slice-start.1
  (41 other events, 83.9 us)
Sparse Core Ops, SparseCore 0:
  15.1 29.8 all-gather.4
  85.8 26.0 reduce-scatter.4
  116.3 27.2 all-gather.6
  145.6 27.2 all-gather.8
  198.4 26.0 reduce-scatter.8
  227.1 26.0 reduce-scatter.6
  260.5 27.2 all-gather.10
  358.7 26.0 reduce-scatter.10
  390.5 259.3 all-reduce.4
